TPU v7x, 32 devices: a whole 2x2x4 slice. The times are simulated.
32 devices in a mesh: seq: 4 (over z), mp: 8 (over y, x, core).
Axes of the slice: x: 2, y: 2, z: 4, core: 2. Of those that a mesh axis runs over, the one named last changes fastest.
Arguments:
- ids: int32 [16, 1024], P('seq'), may hold values from 0 to 274
- lengths: int32 [1024], replicated, may hold values from 1 to 16, 12288 in all
- order: int32 [1024], replicated, may hold values from 0 to 1023, each once
- h_init: bfloat16 [2, 1024, 2048], P(None, 'seq', 'mp'), may hold values from -3 to 3
- c_init: float32 [2, 1024, 2048], P(None, 'seq', 'mp'), may hold values from -5 to 5
- embed: bfloat16 [2, 275, 100], replicated, may hold values from -5 to 5
- w_in: bfloat16 [2, 100, 8192], P(None, None, 'mp'), may hold values from -0.625 to 0.625
- w_rec: bfloat16 [2, 2048, 8192], P(None, None, 'mp'), may hold values from -0.125 to 0.125
- bias: float32 [2, 8192], P(None, 'mp'), may hold values from -3 to 3
- w_dec: bfloat16 [2, 2048, 275], P(None, 'mp'), may hold values from -0.75 to 0.75
- b_dec: float32 [2, 275], replicated, may hold values from -3 to 3
Outputs:
- loss: float32 [], replicated
- h_init_grad: float32 [2, 1024, 2048], P(None, 'seq', 'mp')
- c_init_grad: float32 [2, 1024, 2048], P(None, 'seq', 'mp')
- embed_grad: float32 [2, 275, 100], replicated
- w_in_grad: float32 [2, 100, 8192], P(None, None, ('mp', 'seq'))
- w_rec_grad: float32 [2, 2048, 8192], P(None, 'seq', 'mp')
- bias_grad: float32 [2, 8192], P(None, ('mp', 'seq'))
- w_dec_grad: float32 [2, 2048, 275], P(None, ('mp', 'seq'))
- b_dec_grad: float32 [2, 275], replicated
- rms_embed: float32 [2], replicated
- rms_hidden: float32 [2], replicated
- rms_logits: float32 [2], replicated
Inputs may be any that keep to these rules, and one draw needn't show every extreme that they name: `lengths`: they add up to 12288, and the longest stream is valid over all 16 positions. `order`: every stream stands in exactly one slot.
All inputs are finite; a program needn't handle non-finite values.
Results may differ from a plain program's by a relative error of at most 0.018.
Values may be sent and summed in bfloat16 or wider, within the bound.
A program may use at most 256 MiB of HBM per device.

v0:
```python
import jax
import jax.numpy as jnp
from jax import lax
from jax.sharding import PartitionSpec as P


def extended(x, sides, width):
    for axis, dim in sides:
        peers, length = (lax.axis_size(axis), x.shape[dim])
        up = [(i, (i + 1) % peers) for i in range(peers - 1)]
        down = [(j, i) for i, j in up]
        last = lax.slice_in_dim(x, length - width, length, axis=dim)
        leading = lax.slice_in_dim(x, 0, width, axis=dim)
        before = lax.ppermute(last, axis, up)
        after = lax.ppermute(leading, axis, down)
        x = jnp.concatenate([before, x, after], axis=dim)
    return x


def split_gates(pre_gate):
    grouped = pre_gate.reshape(pre_gate.shape[:-1] + (pre_gate.shape[-1] // 4, 4))
    in_gate = jax.nn.sigmoid(grouped[..., 0])
    forget = jax.nn.sigmoid(grouped[..., 1])
    cell_gate = jnp.tanh(grouped[..., 2])
    out_gate = jax.nn.sigmoid(grouped[..., 3])
    return (in_gate, forget, cell_gate, out_gate)


def per_device(ids, lengths, order, h_init, c_init, embed, w_in, w_rec, bias, w_dec, b_dec):
    seq_count = lax.axis_size("seq")
    mp_count = lax.axis_size("mp")
    seq_rank = lax.axis_index("seq")
    mp_rank = lax.axis_index("mp")
    local_time, streams = ids.shape
    length = local_time * seq_count
    per_dev = streams // seq_count
    letter_count = embed.shape[1]
    own_units = w_rec.shape[2] // 4
    all_units = w_rec.shape[1]
    padded = extended(ids, (("seq", 0),), 1)
    slot_pad = jnp.take(padded, order, axis=1)
    slot_ids = slot_pad[1:-1]
    slot_len = jnp.take(lengths, order)
    count = 2.0 * jnp.sum(slot_len - 1).astype(jnp.float32)
    live_total = jnp.sum(slot_len).astype(jnp.float32)
    letters = jnp.arange(letter_count, dtype=jnp.int32)
    onehot = (slot_ids[:, :, None] == letters).astype(jnp.bfloat16)
    letter_rows = jnp.einsum(
        "tbv,dve->tbde", onehot, embed, preferred_element_type=jnp.float32
    ).astype(jnp.bfloat16)
    gates_in = jnp.einsum(
        "tbde,dec->tbdc", letter_rows, w_in, preferred_element_type=jnp.float32
    ).astype(jnp.bfloat16)
    gates_seq = lax.all_to_all(gates_in, "seq", split_axis=1, concat_axis=0, tiled=True)
    own_len = lax.dynamic_slice_in_dim(slot_len, seq_rank * per_dev, per_dev)
    steps = jnp.arange(length, dtype=jnp.int32)

    def step_live(step):
        return jnp.stack([step < own_len, length - 1 - step < own_len])[:, :, None]

    def step_inputs(table, step):
        fore = lax.dynamic_index_in_dim(table, step, 0, keepdims=False)[:, 0]
        back = lax.dynamic_index_in_dim(table, length - 1 - step, 0, keepdims=False)[:, 1]
        return jnp.stack([fore, back])

    def forward_step(carry, step):
        hidden, cell = carry
        whole = lax.all_gather(hidden, "mp", axis=2, tiled=True)
        recurrent = jnp.einsum("dbh,dhc->dbc", whole, w_rec, preferred_element_type=jnp.float32)
        pre_gate = step_inputs(gates_seq, step).astype(jnp.float32) + recurrent + bias[:, None]
        in_gate, forget, cell_gate, out_gate = split_gates(pre_gate)
        new_cell = forget * cell + in_gate * cell_gate
        live = step_live(step)
        cell_next = jnp.where(live, new_cell, cell)
        hidden_next = jnp.where(
            live, out_gate * jnp.tanh(new_cell), hidden.astype(jnp.float32)
        ).astype(jnp.bfloat16)
        return ((hidden_next, cell_next), (hidden, cell, pre_gate, hidden_next))

    final_state, (kept_states, cells, pre_gates, outputs) = lax.scan(
        forward_step, (h_init, c_init), steps
    )
    fore_mask = steps[:, None] < own_len[None, :]
    back_mask = (length - 1 - steps)[:, None] < own_len[None, :]
    live_masks = jnp.stack([fore_mask, back_mask], axis=1).astype(jnp.float32)
    outputs_wide = outputs.astype(jnp.float32)
    hidden_sq_part = jnp.sum(live_masks[..., None] * outputs_wide * outputs_wide, axis=(0, 2, 3))
    time_hidden = jnp.stack([outputs[:, 0], jnp.flip(outputs[:, 1], 0)], axis=2)
    time_major = lax.all_to_all(time_hidden, "seq", split_axis=0, concat_axis=1, tiled=True)
    rows = local_time * streams
    token_hidden = time_major.reshape(rows, 2, own_units)
    tok_dev = rows // mp_count
    piece = token_hidden
    logits = (
        lax.psum_scatter(
            jnp.einsum("rdh,dhv->rdv", piece, w_dec, preferred_element_type=jnp.float32).astype(
                jnp.bfloat16
            ),
            "mp",
            scatter_dimension=0,
            tiled=True,
        ).astype(jnp.float32)
        + b_dec[None]
    )
    first = mp_rank * tok_dev
    ahead = lax.dynamic_slice_in_dim(slot_pad[2:].reshape(rows), first, tok_dev)
    behind = lax.dynamic_slice_in_dim(slot_pad[:-2].reshape(rows), first, tok_dev)
    time_grid = seq_rank * local_time + jnp.arange(local_time, dtype=jnp.int32)[:, None]
    time_rows = lax.dynamic_slice_in_dim(
        jnp.broadcast_to(time_grid, (local_time, streams)).reshape(rows), first, tok_dev
    )
    len_rows = lax.dynamic_slice_in_dim(
        jnp.broadcast_to(slot_len[None, :], (local_time, streams)).reshape(rows), first, tok_dev
    )
    fore_valid = time_rows + 1 < len_rows
    back_valid = (time_rows >= 1) & (time_rows < len_rows)
    valid = jnp.stack([fore_valid, back_valid], axis=1).astype(jnp.float32)
    targets = jnp.stack([ahead, behind], axis=1)
    logit_sq_part = jnp.sum(valid[:, :, None] * logits * logits, axis=(0, 2))
    top = jnp.max(logits, axis=-1, keepdims=True)
    total = jnp.sum(jnp.exp(logits - top), axis=-1, keepdims=True)
    log_total = top + jnp.log(total)
    softmax_out = jnp.exp(logits - log_total)
    target_hot = targets[:, :, None] == letters
    picked = jnp.sum(jnp.where(target_hot, logits, 0.0), axis=-1)
    loss_part = jnp.sum(valid * (log_total[:, :, 0] - picked))
    grad_logits = (
        valid[:, :, None] * (softmax_out - target_hot.astype(jnp.float32)) / count
    ).astype(jnp.bfloat16)
    dec_bias_part = jnp.sum(grad_logits.astype(jnp.float32), axis=0)
    piece = lax.all_gather(grad_logits, "mp", axis=0, tiled=True)
    grad_piece = jnp.einsum("rdv,dhv->rdh", piece, w_dec, preferred_element_type=jnp.float32)
    grad_dec = jnp.einsum("rdh,rdv->dhv", token_hidden, piece, preferred_element_type=jnp.float32)
    grad_from_dec = lax.all_to_all(
        grad_piece.reshape(local_time, streams, 2, own_units).astype(jnp.bfloat16),
        "seq",
        split_axis=1,
        concat_axis=0,
        tiled=True,
    ).astype(jnp.float32)

    def backward_step(carry, inputs):
        grad_hidden, grad_cell = carry
        step, cell, pre_gate = inputs
        grad_hidden = grad_hidden + step_inputs(grad_from_dec, step)
        in_gate, forget, cell_gate, out_gate = split_gates(pre_gate)
        new_cell = forget * cell + in_gate * cell_gate
        squash = jnp.tanh(new_cell)
        live = step_live(step)
        grad_new = jnp.where(
            live, grad_cell + grad_hidden * out_gate * (1.0 - squash * squash), 0.0
        )
        grad_out = jnp.where(live, grad_hidden * squash, 0.0)
        grad_stack = jnp.stack(
            [
                grad_new * cell_gate * in_gate * (1.0 - in_gate),
                grad_new * cell * forget * (1.0 - forget),
                grad_new * in_gate * (1.0 - cell_gate * cell_gate),
                grad_out * out_gate * (1.0 - out_gate),
            ],
            axis=-1,
        )
        grad_pre = grad_stack.reshape(pre_gate.shape).astype(jnp.bfloat16)
        grad_cell_prev = grad_new * forget + jnp.where(live, 0.0, grad_cell)
        held = jnp.where(live, 0.0, grad_hidden)
        terms = jnp.einsum("dbc,dhc->dbh", grad_pre, w_rec, preferred_element_type=jnp.float32)
        through = lax.psum_scatter(
            terms.astype(jnp.bfloat16), "mp", scatter_dimension=2, tiled=True
        ).astype(jnp.float32)
        return ((held + through, grad_cell_prev), grad_pre)

    start_state = jnp.zeros(c_init.shape, jnp.float32)
    (hidden_grad, cell_grad), grad_pres = lax.scan(
        backward_step, (start_state, start_state), (steps, cells, pre_gates), reverse=True
    )
    rec_grad = jnp.einsum(
        "sdbh,sdbc->dhc",
        lax.all_gather(kept_states, "mp", axis=3, tiled=True),
        grad_pres,
        preferred_element_type=jnp.float32,
    )
    gate_bias_grad = jnp.sum(grad_pres.astype(jnp.float32), axis=(0, 2))
    grad_time = jnp.stack([grad_pres[:, 0], jnp.flip(grad_pres[:, 1], 0)], axis=2)
    grad_major = lax.all_to_all(grad_time, "seq", split_axis=0, concat_axis=1, tiled=True)
    in_grad = jnp.einsum(
        "tbde,tbdc->dec", letter_rows, grad_major, preferred_element_type=jnp.float32
    )
    letter_grad = jnp.einsum(
        "tbv,tbdc->dvc", onehot, grad_major, preferred_element_type=jnp.float32
    )
    embed_part = jnp.einsum(
        "dvc,dec->dve", letter_grad, w_in.astype(jnp.float32), precision=lax.Precision.HIGHEST
    )
    rec_part, bias_part, in_part, dec_part = (
        lax.psum_scatter(
            rec_grad.astype(jnp.bfloat16), "seq", scatter_dimension=1, tiled=True
        ).astype(jnp.float32),
        lax.psum_scatter(
            gate_bias_grad.astype(jnp.bfloat16), "seq", scatter_dimension=1, tiled=True
        ).astype(jnp.float32),
        lax.psum_scatter(
            in_grad.astype(jnp.bfloat16), "seq", scatter_dimension=2, tiled=True
        ).astype(jnp.float32),
        lax.psum_scatter(
            grad_dec.astype(jnp.bfloat16), "seq", scatter_dimension=1, tiled=True
        ).astype(jnp.float32),
    )
    loss_sum, hidden_sq, logit_sq, dec_bias_grad, embed_grad = lax.psum(
        (loss_part, hidden_sq_part, logit_sq_part, dec_bias_part, embed_part), ("seq", "mp")
    )
    embed_wide = embed.astype(jnp.float32)
    rms_embed = jnp.sqrt(jnp.mean(embed_wide * embed_wide, axis=(1, 2)))
    rms_hidden = jnp.sqrt(hidden_sq / (all_units * live_total))
    rms_logits = jnp.sqrt(logit_sq / (letter_count * count / 2.0))
    return (
        loss_sum / count,
        hidden_grad,
        cell_grad,
        embed_grad,
        in_part,
        rec_part,
        bias_part,
        dec_part,
        dec_bias_grad,
        rms_embed,
        rms_hidden,
        rms_logits,
    )


def solution(mesh):
    in_specs = (
        P("seq", None),
        P(),
        P(),
        P(None, "seq", "mp"),
        P(None, "seq", "mp"),
        P(),
        P(None, None, "mp"),
        P(None, None, "mp"),
        P(None, "mp"),
        P(None, "mp", None),
        P(),
    )
    out_specs = (
        P(),
        P(None, "seq", "mp"),
        P(None, "seq", "mp"),
        P(),
        P(None, None, ("mp", "seq")),
        P(None, "seq", "mp"),
        P(None, ("mp", "seq")),
        P(None, ("mp", "seq"), None),
        P(),
        P(),
        P(),
        P(),
    )
    return jax.shard_map(
        per_device, mesh=mesh, in_specs=in_specs, out_specs=out_specs, check_vma=False
    )
```

profile of v0, /device:TPU:0, one launch (start us, length us, event | category | flops | bytes accessed | tf_op | source)
XLA Modules:
  0.0 3546.5 jit_solution(18025429574799147192)
XLA Ops:
  27.3 8.2 convert_bitcast_fusion
  35.5 22.1 copy.205
  65.6 362.8 %all-to-all-done = bf16[4,1024,2,1024]{3,0,2,1:T(4,128)(2,1)} async-done(((bf16[4,1024,2,1024]{3,0,2,1:T(4,128)(2,1)}), bf16[4,1024,2,1024]{3,0,2,1:T(4,128)(2,1)}, u32[]{:S(2)}, u32[]{:S(2)}) %all-to-all-start) | async-done | bytes 16777248 | tf_op jit(solution)/shard_map/all_to_all | solution.py:54
  428.4 17.1 copy.206
  446.1 767.4 %while.41 = (s32[]{:T(128)}, bf16[2,256,256]{2,1,0:T(8,128)(2,1)S(1)}, f32[2,256,256]{2,1,0:T(8,128)S(1)}, bf16[16,2,256,256]{2,3,0,1:T(8,128)(2,1)}, f32[16,2,2...) while((s32[]{:T(128)}, ...), condition=%wide.region_1.2_spmd, body=%wide.region_0.1_spmd.sunk | while | flops 2152858624 | bytes 51395484 | solution.py:80
  458.5 18.1 all-gather.8.cloned.1.call-done
  505.7 19.0 all-gather.8.cloned.1.call-done
  553.9 19.1 all-gather.8.cloned.1.call-done
  573.0 7.8 bitcast_dynamic-update-slice_fusion.6
  602.1 18.8 all-gather.8.cloned.1.call-done
  620.9 7.8 bitcast_dynamic-update-slice_fusion.6
  650.0 18.8 all-gather.8.cloned.1.call-done
  668.8 7.8 bitcast_dynamic-update-slice_fusion.6
  697.9 18.8 all-gather.8.cloned.1.call-done
  716.6 7.8 bitcast_dynamic-update-slice_fusion.6
  745.8 19.1 all-gather.8.cloned.1.call-done
  793.9 19.1 all-gather.8.cloned.1.call-done
  842.0 19.1 all-gather.8.cloned.1.call-done
  890.2 18.8 all-gather.8.cloned.1.call-done
  938.1 19.1 all-gather.8.cloned.1.call-done
  957.1 7.8 bitcast_dynamic-update-slice_fusion.6
  986.3 18.8 all-gather.8.cloned.1.call-done
  1005.1 7.8 bitcast_dynamic-update-slice_fusion.6
  1034.2 19.1 all-gather.8.cloned.1.call-done
  1053.3 7.8 bitcast_dynamic-update-slice_fusion.6
  1082.4 18.8 all-gather.8.cloned.1.call-done
  1130.3 18.7 all-gather.8.cloned.1.call-done
  1178.1 18.8 all-gather.8.cloned.1.call-done
  1216.6 98.0 %all_to_all.60 = bf16[16,256,2,256]{3,1,2,0:T(8,128)(2,1)S(1)} all-to-all(bf16[16,256,2,256]{3,1,2,0:T(8,128)(2,1)S(1)} %pad_maximum_fusion.1), channel_id=1, replica_groups=mesh['seq'=4,'mp'=8] {'seq'}, dimensions={0} | all-to-all | bytes 8388608 | tf_op jit(solution)/shard_map/all_to_all | solution.py:89
  1322.7 49.4 %reduce-scatter.9.cloned.1.call-done = bf16[512,2,275]{0,2,1:T(8,128)(2,1)} async-done(((bf16[4096,2,275]{0,2,1:T(8,128)(2,1)}), bf16[512,2,275]{0,2,1:T(8,128)(2,1)}) %reduce-scatter.9.cloned.1.call-update) | async-done | bytes 563216 | tf_op jit(solution)/shard_map/reduce_scatter | solution.py:95
  1379.3 39.1 %all-gather.4.cloned.1.call-done = bf16[4096,2,275]{0,2,1:T(8,128)(2,1)} async-done(((bf16[512,2,275]{0,2,1:T(8,128)(2,1)}), bf16[4096,2,275]{0,2,1:T(8,128)(2,1)}) %all-gather.4.cloned.1.call-update) | async-done | bytes 4505616 | tf_op jit(solution)/shard_map/all_gather | solution.py:131
  1433.9 93.9 %all-to-all-done.2 = bf16[4,1024,2,256]{3,0,2,1:T(4,128)(2,1)} async-done(((bf16[4,1024,2,256]{3,0,2,1:T(4,128)(2,1)}), bf16[4,1024,2,256]{3,0,2,1:T(4,128)(2,1)}, u32[]{:S(2)}, u32[]{:S(2)}) %all-to-all-start.2) | async-done | bytes 4194336 | tf_op jit(solution)/shard_map/all_to_all | solution.py:134
  1537.5 10.1 broadcast_in_dim.156
  1547.6 1216.8 %while.42 = (s32[]{:T(128)}, f32[2,256,256]{2,1,0:T(8,128)}, f32[2,256,256]{2,1,0:T(8,128)}, bf16[16,2,256,1024]{2,1,3,0:T(2,128)(2,1)}, s32[16]{0:T(128)}, /*in...) while((s32[]{:T(128)}, f32[2,256,256]{2,1,0:T(8,128)}, ...), condition=%wide.region_11.12_spmd.clone, body=%wide.region_9.11_spmd.clone.sunk | while | flops 2157708288 | bytes 57681272 | solution.py:173
  1581.9 37.7 %reduce-scatter.19.cloned.1.call-done = bf16[2,256,256]{2,1,0:T(8,128)(2,1)} async-done(((bf16[2,256,2048]{2,1,0:T(8,128)(2,1)}), bf16[2,256,256]{2,1,0:T(8,128)(2,1)}) %reduce-scatter.19.cloned.1.call-update) | async-done | bytes 262160 | tf_op jit(solution)/shard_map/while/body/eval_jaxpr/reduce_scatter | solution.py:167
  1656.2 39.7 %reduce-scatter.19.cloned.1.call-done = bf16[2,256,256]{2,1,0:T(8,128)(2,1)} async-done(((bf16[2,256,2048]{2,1,0:T(8,128)(2,1)}), bf16[2,256,256]{2,1,0:T(8,128)(2,1)}) %reduce-scatter.19.cloned.1.call-update) | async-done | bytes 262160 | tf_op jit(solution)/shard_map/while/body/eval_jaxpr/reduce_scatter | solution.py:167
  1732.4 39.6 %reduce-scatter.19.cloned.1.call-done = bf16[2,256,256]{2,1,0:T(8,128)(2,1)} async-done(((bf16[2,256,2048]{2,1,0:T(8,128)(2,1)}), bf16[2,256,256]{2,1,0:T(8,128)(2,1)}) %reduce-scatter.19.cloned.1.call-update) | async-done | bytes 262160 | tf_op jit(solution)/shard_map/while/body/eval_jaxpr/reduce_scatter | solution.py:167
  1808.6 39.6 %reduce-scatter.19.cloned.1.call-done = bf16[2,256,256]{2,1,0:T(8,128)(2,1)} async-done(((bf16[2,256,2048]{2,1,0:T(8,128)(2,1)}), bf16[2,256,256]{2,1,0:T(8,128)(2,1)}) %reduce-scatter.19.cloned.1.call-update) | async-done | bytes 262160 | tf_op jit(solution)/shard_map/while/body/eval_jaxpr/reduce_scatter | solution.py:167
  1884.8 39.6 %reduce-scatter.19.cloned.1.call-done = bf16[2,256,256]{2,1,0:T(8,128)(2,1)} async-done(((bf16[2,256,2048]{2,1,0:T(8,128)(2,1)}), bf16[2,256,256]{2,1,0:T(8,128)(2,1)}) %reduce-scatter.19.cloned.1.call-update) | async-done | bytes 262160 | tf_op jit(solution)/shard_map/while/body/eval_jaxpr/reduce_scatter | solution.py:167
  1961.0 39.7 %reduce-scatter.19.cloned.1.call-done = bf16[2,256,256]{2,1,0:T(8,128)(2,1)} async-done(((bf16[2,256,2048]{2,1,0:T(8,128)(2,1)}), bf16[2,256,256]{2,1,0:T(8,128)(2,1)}) %reduce-scatter.19.cloned.1.call-update) | async-done | bytes 262160 | tf_op jit(solution)/shard_map/while/body/eval_jaxpr/reduce_scatter | solution.py:167
  2037.2 39.7 %reduce-scatter.19.cloned.1.call-done = bf16[2,256,256]{2,1,0:T(8,128)(2,1)} async-done(((bf16[2,256,2048]{2,1,0:T(8,128)(2,1)}), bf16[2,256,256]{2,1,0:T(8,128)(2,1)}) %reduce-scatter.19.cloned.1.call-update) | async-done | bytes 262160 | tf_op jit(solution)/shard_map/while/body/eval_jaxpr/reduce_scatter | solution.py:167
  2113.4 39.6 %reduce-scatter.19.cloned.1.call-done = bf16[2,256,256]{2,1,0:T(8,128)(2,1)} async-done(((bf16[2,256,2048]{2,1,0:T(8,128)(2,1)}), bf16[2,256,256]{2,1,0:T(8,128)(2,1)}) %reduce-scatter.19.cloned.1.call-update) | async-done | bytes 262160 | tf_op jit(solution)/shard_map/while/body/eval_jaxpr/reduce_scatter | solution.py:167
  2189.6 39.6 %reduce-scatter.19.cloned.1.call-done = bf16[2,256,256]{2,1,0:T(8,128)(2,1)} async-done(((bf16[2,256,2048]{2,1,0:T(8,128)(2,1)}), bf16[2,256,256]{2,1,0:T(8,128)(2,1)}) %reduce-scatter.19.cloned.1.call-update) | async-done | bytes 262160 | tf_op jit(solution)/shard_map/while/body/eval_jaxpr/reduce_scatter | solution.py:167
  2265.8 39.6 %reduce-scatter.19.cloned.1.call-done = bf16[2,256,256]{2,1,0:T(8,128)(2,1)} async-done(((bf16[2,256,2048]{2,1,0:T(8,128)(2,1)}), bf16[2,256,256]{2,1,0:T(8,128)(2,1)}) %reduce-scatter.19.cloned.1.call-update) | async-done | bytes 262160 | tf_op jit(solution)/shard_map/while/body/eval_jaxpr/reduce_scatter | solution.py:167
  2341.9 39.7 %reduce-scatter.19.cloned.1.call-done = bf16[2,256,256]{2,1,0:T(8,128)(2,1)} async-done(((bf16[2,256,2048]{2,1,0:T(8,128)(2,1)}), bf16[2,256,256]{2,1,0:T(8,128)(2,1)}) %reduce-scatter.19.cloned.1.call-update) | async-done | bytes 262160 | tf_op jit(solution)/shard_map/while/body/eval_jaxpr/reduce_scatter | solution.py:167
  2418.1 39.7 %reduce-scatter.19.cloned.1.call-done = bf16[2,256,256]{2,1,0:T(8,128)(2,1)} async-done(((bf16[2,256,2048]{2,1,0:T(8,128)(2,1)}), bf16[2,256,256]{2,1,0:T(8,128)(2,1)}) %reduce-scatter.19.cloned.1.call-update) | async-done | bytes 262160 | tf_op jit(solution)/shard_map/while/body/eval_jaxpr/reduce_scatter | solution.py:167
  2494.3 39.6 %reduce-scatter.19.cloned.1.call-done = bf16[2,256,256]{2,1,0:T(8,128)(2,1)} async-done(((bf16[2,256,2048]{2,1,0:T(8,128)(2,1)}), bf16[2,256,256]{2,1,0:T(8,128)(2,1)}) %reduce-scatter.19.cloned.1.call-update) | async-done | bytes 262160 | tf_op jit(solution)/shard_map/while/body/eval_jaxpr/reduce_scatter | solution.py:167
  2570.5 39.7 %reduce-scatter.19.cloned.1.call-done = bf16[2,256,256]{2,1,0:T(8,128)(2,1)} async-done(((bf16[2,256,2048]{2,1,0:T(8,128)(2,1)}), bf16[2,256,256]{2,1,0:T(8,128)(2,1)}) %reduce-scatter.19.cloned.1.call-update) | async-done | bytes 262160 | tf_op jit(solution)/shard_map/while/body/eval_jaxpr/reduce_scatter | solution.py:167
  2646.7 39.6 %reduce-scatter.19.cloned.1.call-done = bf16[2,256,256]{2,1,0:T(8,128)(2,1)} async-done(((bf16[2,256,2048]{2,1,0:T(8,128)(2,1)}), bf16[2,256,256]{2,1,0:T(8,128)(2,1)}) %reduce-scatter.19.cloned.1.call-update) | async-done | bytes 262160 | tf_op jit(solution)/shard_map/while/body/eval_jaxpr/reduce_scatter | solution.py:167
  2722.9 39.6 %reduce-scatter.19.cloned.1.call-done = bf16[2,256,256]{2,1,0:T(8,128)(2,1)} async-done(((bf16[2,256,2048]{2,1,0:T(8,128)(2,1)}), bf16[2,256,256]{2,1,0:T(8,128)(2,1)}) %reduce-scatter.19.cloned.1.call-update) | async-done | bytes 262160 | tf_op jit(solution)/shard_map/while/body/eval_jaxpr/reduce_scatter | solution.py:167
  2765.0 41.4 %copy.217 = bf16[16,2,256,1024]{3,2,0,1:T(8,128)(2,1)} copy(bf16[16,2,256,1024]{2,1,3,0:T(2,128)(2,1)} %get-tuple-element.370) | data formatting | bytes 33554432 | tf_op jit(solution)/shard_map/while | solution.py:173
  2806.4 11.6 slice_bitcast_fusion.5
  2818.0 8.0 reverse_bitcast_fusion
  2826.0 8.9 pad_maximum_fusion
  2834.9 8.8 copy.219
  2858.4 18.8 reduce_sum.97
  2877.5 347.3 %all-to-all-done.3 = bf16[16,256,2,1024]{3,1,2,0:T(8,128)(2,1)} async-done(((bf16[16,256,2,1024]{3,1,2,0:T(8,128)(2,1)}), bf16[16,256,2,1024]{3,1,2,0:T(8,128)(2,1)}, u32[]{:S(2)}, u32[]{:S(2)}) %all-to-all-start.3) | async-done | bytes 16777248 | tf_op jit(solution)/shard_map/all_to_all | solution.py:184
  3224.8 8.2 copy.220
  3241.1 9.2 fusion.46
  3250.6 42.5 %bitcast_convert_fusion = bf16[2,2048,1024]{2,1,0:T(8,128)(2,1)} fusion(bf16[16,2,256,2048]{2,3,0,1:T(8,128)(2,1)} %all-gather.6.cloned.1.call-done, bf16[16,2,256,1024]{3,2,0,1:T(8,128)(2,1)} %copy.217), kind=kOutput, calls=%fused_computation.73 | convolution fusion | flops 34363932672 | bytes 58720256 | tf_op jit(solution)/shard_map/sdbh,sdbc->dhc/dot_general | solution.py:176
  3299.3 37.6 %all-reduce = (f32[]{:T(128)}, f32[2,275]{1,0:T(2,128)}, f32[2]{0:T(128)S(1)}, f32[2]{0:T(128)S(1)}) all-reduce(f32[]{:T(128)} %get-tuple-element.605, f32[2,275]{1,0:T(2,128)S(1)} %copy-done.25, f32[2]{0:T(128)S(1)} %fusion.27, f32[2]{0:T(128)S(1)} %copy-done.26), channel_id=1, replica_groups=mesh['seq'=4,'mp'=8] {'seq','mp'}, use_global_device_ids=true, to_apply=%region_7.8 | all-reduce | flops 555 | bytes 4440 | tf_op jit(solution)/shard_map/psum | solution.py:208
  3341.6 23.3 all-reduce.3.cloned.1.call-done
  3366.7 22.2 reduce-scatter.11.cloned.1.call-done
  3390.6 143.3 %reduce-scatter.13.cloned.1.call-done = bf16[2,512,1024]{2,1,0:T(8,128)(2,1)} async-done(((bf16[2,2048,1024]{2,1,0:T(8,128)(2,1)}), bf16[2,512,1024]{2,1,0:T(8,128)(2,1)}) %reduce-scatter.13.cloned.1.call-update) | async-done | bytes 2097168 | tf_op jit(solution)/shard_map/reduce_scatter | solution.py:195
  (1008 shorter events, 996.2 us)
Async XLA Ops:
  8.0 19.3 copy-start
  8.9 12.1 collective-permute-start
  13.8 7.2 collective-permute-start.1
  21.0 44.0 %copy-start.20 = (s32[1024]{0:T(1024)}, s32[1024]{0:T(1024)S(1)}, u32[]{:S(2)}) copy-start(s32[1024]{0:T(1024)S(1)} %get-tuple-element.603) | copy-start | bytes 12292
  57.6 370.8 %all-to-all-start = ((bf16[4,1024,2,1024]{3,0,2,1:T(4,128)(2,1)}), bf16[4,1024,2,1024]{3,0,2,1:T(4,128)(2,1)}, u32[]{:S(2)}, u32[]{:S(2)}) async-start(bf16[4,1024,2,1024]{3,0,2,1:T(4,128)(2,1)} %copy.205), calls=%async_computation.1 | async-start | bytes 33554432 | tf_op jit(solution)/shard_map/all_to_all | solution.py:54
  446.1 30.5 all-gather.8.cloned.1.call-start
  493.3 31.5 all-gather.8.cloned.1.call-start
  541.4 31.5 all-gather.8.cloned.1.call-start
  589.7 31.2 all-gather.8.cloned.1.call-start
  637.6 31.2 all-gather.8.cloned.1.call-start
  685.4 31.2 all-gather.8.cloned.1.call-start
  733.3 31.5 all-gather.8.cloned.1.call-start
  781.5 31.5 all-gather.8.cloned.1.call-start
  829.6 31.5 all-gather.8.cloned.1.call-start
  877.8 31.2 all-gather.8.cloned.1.call-start
  925.6 31.5 all-gather.8.cloned.1.call-start
  973.9 31.2 all-gather.8.cloned.1.call-start
  1021.8 31.5 all-gather.8.cloned.1.call-start
  1069.9 31.2 all-gather.8.cloned.1.call-start
  1117.8 31.2 all-gather.8.cloned.1.call-start
  1165.7 31.2 all-gather.8.cloned.1.call-start
  1213.5 158.6 %reduce-scatter.9.cloned.1.call-start = ((), (), s32[]{:S(2)}) async-start(), calls=%async_computation.10 | async-start | bytes 5160960 | tf_op jit(solution)/shard_map/reduce_scatter | solution.py:95
  1320.7 51.4 %copy-start.19 = (f32[2,275]{1,0:T(2,128)S(1)}, f32[2,275]{1,0:T(2,128)}, u32[]{:S(2)}) copy-start(f32[2,275]{1,0:T(2,128)} %param.25) | copy-start | bytes 6604
  1320.7 97.7 %all-gather.4.cloned.1.call-start = ((), (), s32[]{:S(2)}) async-start(), calls=%async_computation.11 | async-start | bytes 5160960 | tf_op jit(solution)/shard_map/all_gather | solution.py:131
  1428.7 99.0 %all-to-all-start.2 = ((bf16[4,1024,2,256]{3,0,2,1:T(4,128)(2,1)}), bf16[4,1024,2,256]{3,0,2,1:T(4,128)(2,1)}, u32[]{:S(2)}, u32[]{:S(2)}) async-start(bf16[4,1024,2,256]{3,0,2,1:T(4,128)(2,1)} %copy.214), calls=%async_computation.4 | async-start | bytes 8388608 | tf_op jit(solution)/shard_map/all_to_all | solution.py:134
  1547.6 72.1 %reduce-scatter.19.cloned.1.call-start = ((), (), s32[]{:S(2)}) async-start(), calls=%async_computation.19 | async-start | bytes 2359296 | tf_op jit(solution)/shard_map/while/body/eval_jaxpr/reduce_scatter | solution.py:167
  1580.2 39.5 %copy-start.14 = (pred[2,256]{1,0:T(4,128)(4,1)S(1)}, pred[2,256]{1,0:T(4,128)(4,1)}, u32[]{:S(2)}) copy-start(pred[2,256]{1,0:T(4,128)(4,1)} %copy-done.13) | copy-start | bytes 1540 | tf_op jit(solution)/shard_map/while
  1621.6 74.3 %reduce-scatter.19.cloned.1.call-start = ((), (), s32[]{:S(2)}) async-start(), calls=%async_computation.19 | async-start | bytes 2359296 | tf_op jit(solution)/shard_map/while/body/eval_jaxpr/reduce_scatter | solution.py:167
  1654.5 41.4 %copy-start.14 = (pred[2,256]{1,0:T(4,128)(4,1)S(1)}, pred[2,256]{1,0:T(4,128)(4,1)}, u32[]{:S(2)}) copy-start(pred[2,256]{1,0:T(4,128)(4,1)} %copy-done.13) | copy-start | bytes 1540 | tf_op jit(solution)/shard_map/while
  1697.8 74.3 %reduce-scatter.19.cloned.1.call-start = ((), (), s32[]{:S(2)}) async-start(), calls=%async_computation.19 | async-start | bytes 2359296 | tf_op jit(solution)/shard_map/while/body/eval_jaxpr/reduce_scatter | solution.py:167
  1730.7 41.4 %copy-start.14 = (pred[2,256]{1,0:T(4,128)(4,1)S(1)}, pred[2,256]{1,0:T(4,128)(4,1)}, u32[]{:S(2)}) copy-start(pred[2,256]{1,0:T(4,128)(4,1)} %copy-done.13) | copy-start | bytes 1540 | tf_op jit(solution)/shard_map/while
  1773.9 74.3 %reduce-scatter.19.cloned.1.call-start = ((), (), s32[]{:S(2)}) async-start(), calls=%async_computation.19 | async-start | bytes 2359296 | tf_op jit(solution)/shard_map/while/body/eval_jaxpr/reduce_scatter | solution.py:167
  1806.9 41.4 %copy-start.14 = (pred[2,256]{1,0:T(4,128)(4,1)S(1)}, pred[2,256]{1,0:T(4,128)(4,1)}, u32[]{:S(2)}) copy-start(pred[2,256]{1,0:T(4,128)(4,1)} %copy-done.13) | copy-start | bytes 1540 | tf_op jit(solution)/shard_map/while
  1850.1 74.3 %reduce-scatter.19.cloned.1.call-start = ((), (), s32[]{:S(2)}) async-start(), calls=%async_computation.19 | async-start | bytes 2359296 | tf_op jit(solution)/shard_map/while/body/eval_jaxpr/reduce_scatter | solution.py:167
  1883.1 41.4 %copy-start.14 = (pred[2,256]{1,0:T(4,128)(4,1)S(1)}, pred[2,256]{1,0:T(4,128)(4,1)}, u32[]{:S(2)}) copy-start(pred[2,256]{1,0:T(4,128)(4,1)} %copy-done.13) | copy-start | bytes 1540 | tf_op jit(solution)/shard_map/while
  1926.3 74.3 %reduce-scatter.19.cloned.1.call-start = ((), (), s32[]{:S(2)}) async-start(), calls=%async_computation.19 | async-start | bytes 2359296 | tf_op jit(solution)/shard_map/while/body/eval_jaxpr/reduce_scatter | solution.py:167
  1959.2 41.4 %copy-start.14 = (pred[2,256]{1,0:T(4,128)(4,1)S(1)}, pred[2,256]{1,0:T(4,128)(4,1)}, u32[]{:S(2)}) copy-start(pred[2,256]{1,0:T(4,128)(4,1)} %copy-done.13) | copy-start | bytes 1540 | tf_op jit(solution)/shard_map/while
  2002.5 74.3 %reduce-scatter.19.cloned.1.call-start = ((), (), s32[]{:S(2)}) async-start(), calls=%async_computation.19 | async-start | bytes 2359296 | tf_op jit(solution)/shard_map/while/body/eval_jaxpr/reduce_scatter | solution.py:167
  2035.4 41.4 %copy-start.14 = (pred[2,256]{1,0:T(4,128)(4,1)S(1)}, pred[2,256]{1,0:T(4,128)(4,1)}, u32[]{:S(2)}) copy-start(pred[2,256]{1,0:T(4,128)(4,1)} %copy-done.13) | copy-start | bytes 1540 | tf_op jit(solution)/shard_map/while
  2078.7 74.3 %reduce-scatter.19.cloned.1.call-start = ((), (), s32[]{:S(2)}) async-start(), calls=%async_computation.19 | async-start | bytes 2359296 | tf_op jit(solution)/shard_map/while/body/eval_jaxpr/reduce_scatter | solution.py:167
  2111.6 41.4 %copy-start.14 = (pred[2,256]{1,0:T(4,128)(4,1)S(1)}, pred[2,256]{1,0:T(4,128)(4,1)}, u32[]{:S(2)}) copy-start(pred[2,256]{1,0:T(4,128)(4,1)} %copy-done.13) | copy-start | bytes 1540 | tf_op jit(solution)/shard_map/while
  2154.9 74.3 %reduce-scatter.19.cloned.1.call-start = ((), (), s32[]{:S(2)}) async-start(), calls=%async_computation.19 | async-start | bytes 2359296 | tf_op jit(solution)/shard_map/while/body/eval_jaxpr/reduce_scatter | solution.py:167
  2187.8 41.4 %copy-start.14 = (pred[2,256]{1,0:T(4,128)(4,1)S(1)}, pred[2,256]{1,0:T(4,128)(4,1)}, u32[]{:S(2)}) copy-start(pred[2,256]{1,0:T(4,128)(4,1)} %copy-done.13) | copy-start | bytes 1540 | tf_op jit(solution)/shard_map/while
  2231.1 74.3 %reduce-scatter.19.cloned.1.call-start = ((), (), s32[]{:S(2)}) async-start(), calls=%async_computation.19 | async-start | bytes 2359296 | tf_op jit(solution)/shard_map/while/body/eval_jaxpr/reduce_scatter | solution.py:167
  2264.0 41.4 %copy-start.14 = (pred[2,256]{1,0:T(4,128)(4,1)S(1)}, pred[2,256]{1,0:T(4,128)(4,1)}, u32[]{:S(2)}) copy-start(pred[2,256]{1,0:T(4,128)(4,1)} %copy-done.13) | copy-start | bytes 1540 | tf_op jit(solution)/shard_map/while
  2307.3 74.3 %reduce-scatter.19.cloned.1.call-start = ((), (), s32[]{:S(2)}) async-start(), calls=%async_computation.19 | async-start | bytes 2359296 | tf_op jit(solution)/shard_map/while/body/eval_jaxpr/reduce_scatter | solution.py:167
  2340.2 41.4 %copy-start.14 = (pred[2,256]{1,0:T(4,128)(4,1)S(1)}, pred[2,256]{1,0:T(4,128)(4,1)}, u32[]{:S(2)}) copy-start(pred[2,256]{1,0:T(4,128)(4,1)} %copy-done.13) | copy-start | bytes 1540 | tf_op jit(solution)/shard_map/while
  2383.5 74.3 %reduce-scatter.19.cloned.1.call-start = ((), (), s32[]{:S(2)}) async-start(), calls=%async_computation.19 | async-start | bytes 2359296 | tf_op jit(solution)/shard_map/while/body/eval_jaxpr/reduce_scatter | solution.py:167
  2416.4 41.4 %copy-start.14 = (pred[2,256]{1,0:T(4,128)(4,1)S(1)}, pred[2,256]{1,0:T(4,128)(4,1)}, u32[]{:S(2)}) copy-start(pred[2,256]{1,0:T(4,128)(4,1)} %copy-done.13) | copy-start | bytes 1540 | tf_op jit(solution)/shard_map/while
  2459.6 74.3 %reduce-scatter.19.cloned.1.call-start = ((), (), s32[]{:S(2)}) async-start(), calls=%async_computation.19 | async-start | bytes 2359296 | tf_op jit(solution)/shard_map/while/body/eval_jaxpr/reduce_scatter | solution.py:167
  2492.6 41.4 %copy-start.14 = (pred[2,256]{1,0:T(4,128)(4,1)S(1)}, pred[2,256]{1,0:T(4,128)(4,1)}, u32[]{:S(2)}) copy-start(pred[2,256]{1,0:T(4,128)(4,1)} %copy-done.13) | copy-start | bytes 1540 | tf_op jit(solution)/shard_map/while
  2535.8 74.3 %reduce-scatter.19.cloned.1.call-start = ((), (), s32[]{:S(2)}) async-start(), calls=%async_computation.19 | async-start | bytes 2359296 | tf_op jit(solution)/shard_map/while/body/eval_jaxpr/reduce_scatter | solution.py:167
  2568.7 41.4 %copy-start.14 = (pred[2,256]{1,0:T(4,128)(4,1)S(1)}, pred[2,256]{1,0:T(4,128)(4,1)}, u32[]{:S(2)}) copy-start(pred[2,256]{1,0:T(4,128)(4,1)} %copy-done.13) | copy-start | bytes 1540 | tf_op jit(solution)/shard_map/while
  2612.0 74.3 %reduce-scatter.19.cloned.1.call-start = ((), (), s32[]{:S(2)}) async-start(), calls=%async_computation.19 | async-start | bytes 2359296 | tf_op jit(solution)/shard_map/while/body/eval_jaxpr/reduce_scatter | solution.py:167
  2644.9 41.4 %copy-start.14 = (pred[2,256]{1,0:T(4,128)(4,1)S(1)}, pred[2,256]{1,0:T(4,128)(4,1)}, u32[]{:S(2)}) copy-start(pred[2,256]{1,0:T(4,128)(4,1)} %copy-done.13) | copy-start | bytes 1540 | tf_op jit(solution)/shard_map/while
  2688.2 74.3 %reduce-scatter.19.cloned.1.call-start = ((), (), s32[]{:S(2)}) async-start(), calls=%async_computation.19 | async-start | bytes 2359296 | tf_op jit(solution)/shard_map/while/body/eval_jaxpr/reduce_scatter | solution.py:167
  2721.1 41.4 %copy-start.14 = (pred[2,256]{1,0:T(4,128)(4,1)S(1)}, pred[2,256]{1,0:T(4,128)(4,1)}, u32[]{:S(2)}) copy-start(pred[2,256]{1,0:T(4,128)(4,1)} %copy-done.13) | copy-start | bytes 1540 | tf_op jit(solution)/shard_map/while
  2764.4 486.2 %all-gather.6.cloned.1.call-start = ((), (), s32[]{:S(2)}) async-start(), calls=%async_computation.14 | async-start | bytes 37748736 | tf_op jit(solution)/shard_map/all_gather | solution.py:178
  2843.8 381.0 %all-to-all-start.3 = ((bf16[16,256,2,1024]{3,1,2,0:T(8,128)(2,1)}), bf16[16,256,2,1024]{3,1,2,0:T(8,128)(2,1)}, u32[]{:S(2)}, u32[]{:S(2)}) async-start(bf16[16,256,2,1024]{3,1,2,0:T(8,128)(2,1)} %copy.219), calls=%async_computation.5 | async-start | bytes 33554432 | tf_op jit(solution)/shard_map/all_to_all | solution.py:184
  2851.0 487.5 %reduce-scatter.15.cloned.1.call-start = ((), (), s32[]{:S(2)}) async-start(), calls=%async_computation.16 | async-start | bytes 491520 | tf_op jit(solution)/shard_map/reduce_scatter | solution.py:204
  2858.3 481.8 %reduce-scatter.17.cloned.1.call-start = ((), (), s32[]{:S(2)}) async-start(), calls=%async_computation.17 | async-start | bytes 327680
  2877.2 487.7 %all-reduce.3.cloned.1.call-start = ((), (), s32[]{:S(2)}) async-start(), calls=%async_computation.12 | async-start | bytes 573440 | tf_op jit(solution)/shard_map/psum | solution.py:208
  3241.1 147.9 %reduce-scatter.11.cloned.1.call-start = ((), (), s32[]{:S(2)}) async-start(), calls=%async_computation.13 | async-start | bytes 532480 | tf_op jit(solution)/shard_map/reduce_scatter | solution.py:201
  3250.3 283.6 %reduce-scatter.13.cloned.1.call-start = ((), (), s32[]{:S(2)}) async-start(), calls=%async_computation.15 | async-start | bytes 10485760 | tf_op jit(solution)/shard_map/reduce_scatter | solution.py:195
  (83 other events, 381.1 us)
Sparse Core Ops, SparseCore 0:
  449.4 27.2 all-gather.7
  496.6 28.1 all-gather.7
  544.7 28.1 all-gather.7
  592.6 28.1 all-gather.7
  640.5 28.1 all-gather.7
  688.4 28.1 all-gather.7
  736.6 28.1 all-gather.7
  784.8 28.1 all-gather.7
  832.9 28.1 all-gather.7
  880.7 28.1 all-gather.7
  928.9 28.1 all-gather.7
  976.8 28.1 all-gather.7
  1025.1 28.1 all-gather.7
  1072.9 28.1 all-gather.7
  1120.8 28.1 all-gather.7
  1168.6 28.1 all-gather.7
  1580.3 39.3 reduce-scatter.18
  1654.6 41.2 reduce-scatter.18
  1730.8 41.2 reduce-scatter.18
  1807.0 41.2 reduce-scatter.18
  1883.2 41.2 reduce-scatter.18
  1959.4 41.2 reduce-scatter.18
  2035.6 41.2 reduce-scatter.18
  2111.8 41.2 reduce-scatter.18
  2188.0 41.1 reduce-scatter.18
  2264.1 41.1 reduce-scatter.18
  2340.3 41.2 reduce-scatter.18
  2416.5 41.2 reduce-scatter.18
  2492.7 41.2 reduce-scatter.18
  2568.9 41.2 reduce-scatter.18
  2645.1 41.2 reduce-scatter.18
  2721.3 41.2 reduce-scatter.18
Sparse Core Ops, SparseCore 1:
  1320.8 51.3 reduce-scatter.8
  1379.4 38.9 all-gather.3
  2767.3 160.6 all-gather.5
  2930.3 28.1 reduce-scatter.14
  2961.4 191.8 reduce-scatter.16
  3241.2 123.7 all-reduce.2
  3367.2 21.7 reduce-scatter.10
  3391.2 142.7 reduce-scatter.12
where the time goes:
time: 3560 us; the launch traced here: 3550 us
  waiting for transfers between devices  2020 us (57%)
  local copies, waits for them, and re-layouts  670 us (19%)
  matrix products  324 us (9%)
  other arithmetic  243 us (7%)
  blocking collectives  136 us (4%)
  loops' own time  111 us (3%)
    reduce_scatter x16, waiting for transfers between devices, backward_step(): lax.psum_scatter(terms.astype(jnp.bfloat16), 'mp', scatter_dimension=2, t...  632 us
    all_to_all x1, waiting for transfers between devices, per_device(): lax.all_to_all(gates_in, 'seq', split_axis=1, concat_axis=0, tiled=True)  363 us
    all_to_all x1, waiting for transfers between devices, per_device(): lax.all_to_all(grad_time, 'seq', split_axis=0, concat_axis=1, tiled=True)  347 us
    all_gather x16, waiting for transfers between devices, forward_step(): whole = lax.all_gather(hidden, 'mp', axis=2, tiled=True)  302 us
    reduce_scatter x1, waiting for transfers between devices, per_device(): lax.psum_scatter(rec_grad.astype(jnp.bfloat16), 'seq', scatter_dimension=...  143 us
    dot_general x16, matrix products, forward_step(): jnp.einsum('dbh,dhc->dbc', whole, w_rec, preferred_element_type=jnp.float32)  124 us
    dot_general x16, matrix products, backward_step(): jnp.einsum('dbc,dhc->dbh', grad_pre, w_rec, preferred_element_type=jnp.fl...  115 us
    all_to_all x1, blocking collectives, per_device(): lax.all_to_all(time_hidden, 'seq', split_axis=0, concat_axis=1, tiled=True)  98 us
  transfers between devices with their start and end apart: 45, of which 40 were waited for; matrix products, arithmetic and copies ran while one was open for 10% of the time, Pallas kernels for 0%

commit v1 on v0

--- a/solution.py
+++ b/solution.py
@@ -1,7 +1,23 @@
+import functools
 import jax
 import jax.numpy as jnp
 from jax import lax
 from jax.sharding import PartitionSpec as P
+
+
+def thing_point(my_tile, bus_axis, on_dim, dim_no):
+    return jnp.concatenate(
+        lax.all_to_all(
+            jnp.stack(jnp.split(my_tile, lax.axis_size(bus_axis), axis=on_dim), axis=0),
+            bus_axis,
+            split_axis=0,
+            concat_axis=0,
+        ),
+        axis=dim_no,
+    )
+
+
+bring_limits = functools.partial(thing_point, bus_axis="seq", on_dim=1, dim_no=0)
 
 
 def extended(x, sides, width):
@@ -131,12 +147,8 @@
     piece = lax.all_gather(grad_logits, "mp", axis=0, tiled=True)
     grad_piece = jnp.einsum("rdv,dhv->rdh", piece, w_dec, preferred_element_type=jnp.float32)
     grad_dec = jnp.einsum("rdh,rdv->dhv", token_hidden, piece, preferred_element_type=jnp.float32)
-    grad_from_dec = lax.all_to_all(
-        grad_piece.reshape(local_time, streams, 2, own_units).astype(jnp.bfloat16),
-        "seq",
-        split_axis=1,
-        concat_axis=0,
-        tiled=True,
+    grad_from_dec = bring_limits(
+        grad_piece.reshape(local_time, streams, 2, own_units).astype(jnp.bfloat16)
     ).astype(jnp.float32)
 
     def backward_step(carry, inputs):

time: 3560 us -> 3550 us (level)
  no operation moved by 1% of the time
where the time goes in v1:
time: 3550 us; the launch traced here: 3530 us
  waiting for transfers between devices  2020 us (57%)
  local copies, waits for them, and re-layouts  666 us (19%)
  matrix products  324 us (9%)
  other arithmetic  241 us (7%)
  blocking collectives  136 us (4%)
  loops' own time  106 us (3%)
    reduce_scatter x16, waiting for transfers between devices, backward_step(): lax.psum_scatter(terms.astype(jnp.bfloat16), 'mp', scatter_dimension=2, t...  633 us
    all_to_all x1, waiting for transfers between devices, per_device(): lax.all_to_all(gates_in, 'seq', split_axis=1, concat_axis=0, tiled=True)  363 us
    all_to_all x1, waiting for transfers between devices, per_device(): lax.all_to_all(grad_time, 'seq', split_axis=0, concat_axis=1, tiled=True)  347 us
    all_gather x16, waiting for transfers between devices, forward_step(): whole = lax.all_gather(hidden, 'mp', axis=2, tiled=True)  302 us
    reduce_scatter x1, waiting for transfers between devices, per_device(): lax.psum_scatter(rec_grad.astype(jnp.bfloat16), 'seq', scatter_dimension=...  143 us
    dot_general x16, matrix products, forward_step(): jnp.einsum('dbh,dhc->dbc', whole, w_rec, preferred_element_type=jnp.float32)  124 us
    dot_general x16, matrix products, backward_step(): jnp.einsum('dbc,dhc->dbh', grad_pre, w_rec, preferred_element_type=jnp.fl...  115 us
    all_to_all x1, blocking collectives, per_device(): lax.all_to_all(time_hidden, 'seq', split_axis=0, concat_axis=1, tiled=True)  98 us
  transfers between devices with their start and end apart: 45, of which 40 were waited for; matrix products, arithmetic and copies ran while one was open for 10% of the time, Pallas kernels for 0%

profile of v1, /device:TPU:0, one launch (start us, length us, event | category | flops | bytes accessed | tf_op | source)
XLA Modules:
  0.0 3534.5 jit_solution(1994453435625389907)
XLA Ops:
  27.3 8.2 convert_bitcast_fusion
  35.5 22.1 copy.204
  65.6 362.8 %all-to-all-done = bf16[4,1024,2,1024]{3,0,2,1:T(4,128)(2,1)} async-done(((bf16[4,1024,2,1024]{3,0,2,1:T(4,128)(2,1)}), bf16[4,1024,2,1024]{3,0,2,1:T(4,128)(2,1)}, u32[]{:S(2)}, u32[]{:S(2)}) %all-to-all-start) | async-done | bytes 16777248 | tf_op jit(solution)/shard_map/all_to_all | solution.py:70
  428.4 17.1 copy.205
  446.0 767.3 %while.41 = (s32[]{:T(128)}, bf16[2,256,256]{2,1,0:T(8,128)(2,1)S(1)}, f32[2,256,256]{2,1,0:T(8,128)S(1)}, bf16[16,2,256,256]{2,3,0,1:T(8,128)(2,1)}, f32[16,2,2...) while((s32[]{:T(128)}, ...), condition=%wide.region_1.2_spmd, body=%wide.region_0.1_spmd.sunk | while | flops 2152858624 | bytes 51395484 | solution.py:96
  458.5 18.1 all-gather.8.cloned.1.call-done
  505.7 19.0 all-gather.8.cloned.1.call-done
  553.8 19.1 all-gather.8.cloned.1.call-done
  572.9 7.8 bitcast_dynamic-update-slice_fusion.6
  602.0 18.8 all-gather.8.cloned.1.call-done
  620.8 7.8 bitcast_dynamic-update-slice_fusion.6
  649.9 18.8 all-gather.8.cloned.1.call-done
  668.7 7.8 bitcast_dynamic-update-slice_fusion.6
  697.8 18.8 all-gather.8.cloned.1.call-done
  716.6 7.8 bitcast_dynamic-update-slice_fusion.6
  745.7 19.1 all-gather.8.cloned.1.call-done
  793.9 19.1 all-gather.8.cloned.1.call-done
  842.0 19.1 all-gather.8.cloned.1.call-done
  890.1 18.8 all-gather.8.cloned.1.call-done
  938.0 19.1 all-gather.8.cloned.1.call-done
  957.1 7.8 bitcast_dynamic-update-slice_fusion.6
  986.2 18.8 all-gather.8.cloned.1.call-done
  1005.0 7.8 bitcast_dynamic-update-slice_fusion.6
  1034.1 19.0 all-gather.8.cloned.1.call-done
  1082.3 18.8 all-gather.8.cloned.1.call-done
  1101.0 7.8 bitcast_dynamic-update-slice_fusion.6
  1130.2 18.8 all-gather.8.cloned.1.call-done
  1178.0 18.8 all-gather.8.cloned.1.call-done
  1216.5 98.0 %all_to_all.56 = bf16[16,256,2,256]{3,1,2,0:T(8,128)(2,1)S(1)} all-to-all(bf16[16,256,2,256]{3,1,2,0:T(8,128)(2,1)S(1)} %pad_maximum_fusion.1), channel_id=1, replica_groups=mesh['seq'=4,'mp'=8] {'seq'}, dimensions={0} | all-to-all | bytes 8388608 | tf_op jit(solution)/shard_map/all_to_all | solution.py:105
  1322.6 49.4 %reduce-scatter.9.cloned.1.call-done = bf16[512,2,275]{0,2,1:T(8,128)(2,1)} async-done(((bf16[4096,2,275]{0,2,1:T(8,128)(2,1)}), bf16[512,2,275]{0,2,1:T(8,128)(2,1)}) %reduce-scatter.9.cloned.1.call-update) | async-done | bytes 563216 | tf_op jit(solution)/shard_map/reduce_scatter | solution.py:111
  1379.2 39.1 %all-gather.4.cloned.1.call-done = bf16[4096,2,275]{0,2,1:T(8,128)(2,1)} async-done(((bf16[512,2,275]{0,2,1:T(8,128)(2,1)}), bf16[4096,2,275]{0,2,1:T(8,128)(2,1)}) %all-gather.4.cloned.1.call-update) | async-done | bytes 4505616 | tf_op jit(solution)/shard_map/all_gather | solution.py:147
  1430.8 93.9 %all-to-all-done.2 = bf16[4,4,256,2,256]{4,2,1,3,0:T(8,128)(2,1)} async-done(((bf16[4,4,256,2,256]{4,2,1,3,0:T(8,128)(2,1)}), bf16[4,4,256,2,256]{4,2,1,3,0:T(8,128)(2,1)}, u32[]{:S(2)}, u32[]{:S(2)}) %all-to-all-start.2) | async-done | bytes 4194336 | tf_op jit(solution)/shard_map/all_to_all | solution.py:10
  1531.8 10.1 broadcast_in_dim.156
  1541.9 1210.5 %while.42 = (s32[]{:T(128)}, f32[2,256,256]{2,1,0:T(8,128)}, f32[2,256,256]{2,1,0:T(8,128)}, bf16[16,2,256,1024]{2,1,3,0:T(2,128)(2,1)}, s32[16]{0:T(128)}, /*in...) while((s32[]{:T(128)}, f32[2,256,256]{2,1,0:T(8,128)}, ...), condition=%wide.region_11.12_spmd.clone, body=%wide.region_9.11_spmd.clone.sunk | while | flops 2157708288 | bytes 57681272 | solution.py:185
  1575.8 37.8 %reduce-scatter.19.cloned.1.call-done = bf16[2,256,256]{2,1,0:T(8,128)(2,1)} async-done(((bf16[2,256,2048]{2,1,0:T(8,128)(2,1)}), bf16[2,256,256]{2,1,0:T(8,128)(2,1)}) %reduce-scatter.19.cloned.1.call-update) | async-done | bytes 262160 | tf_op jit(solution)/shard_map/while/body/eval_jaxpr/reduce_scatter | solution.py:179
  1649.7 39.7 %reduce-scatter.19.cloned.1.call-done = bf16[2,256,256]{2,1,0:T(8,128)(2,1)} async-done(((bf16[2,256,2048]{2,1,0:T(8,128)(2,1)}), bf16[2,256,256]{2,1,0:T(8,128)(2,1)}) %reduce-scatter.19.cloned.1.call-update) | async-done | bytes 262160 | tf_op jit(solution)/shard_map/while/body/eval_jaxpr/reduce_scatter | solution.py:179
  1725.6 39.6 %reduce-scatter.19.cloned.1.call-done = bf16[2,256,256]{2,1,0:T(8,128)(2,1)} async-done(((bf16[2,256,2048]{2,1,0:T(8,128)(2,1)}), bf16[2,256,256]{2,1,0:T(8,128)(2,1)}) %reduce-scatter.19.cloned.1.call-update) | async-done | bytes 262160 | tf_op jit(solution)/shard_map/while/body/eval_jaxpr/reduce_scatter | solution.py:179
  1801.4 39.6 %reduce-scatter.19.cloned.1.call-done = bf16[2,256,256]{2,1,0:T(8,128)(2,1)} async-done(((bf16[2,256,2048]{2,1,0:T(8,128)(2,1)}), bf16[2,256,256]{2,1,0:T(8,128)(2,1)}) %reduce-scatter.19.cloned.1.call-update) | async-done | bytes 262160 | tf_op jit(solution)/shard_map/while/body/eval_jaxpr/reduce_scatter | solution.py:179
  1877.1 39.6 %reduce-scatter.19.cloned.1.call-done = bf16[2,256,256]{2,1,0:T(8,128)(2,1)} async-done(((bf16[2,256,2048]{2,1,0:T(8,128)(2,1)}), bf16[2,256,256]{2,1,0:T(8,128)(2,1)}) %reduce-scatter.19.cloned.1.call-update) | async-done | bytes 262160 | tf_op jit(solution)/shard_map/while/body/eval_jaxpr/reduce_scatter | solution.py:179
  1952.9 39.7 %reduce-scatter.19.cloned.1.call-done = bf16[2,256,256]{2,1,0:T(8,128)(2,1)} async-done(((bf16[2,256,2048]{2,1,0:T(8,128)(2,1)}), bf16[2,256,256]{2,1,0:T(8,128)(2,1)}) %reduce-scatter.19.cloned.1.call-update) | async-done | bytes 262160 | tf_op jit(solution)/shard_map/while/body/eval_jaxpr/reduce_scatter | solution.py:179
  2028.7 39.7 %reduce-scatter.19.cloned.1.call-done = bf16[2,256,256]{2,1,0:T(8,128)(2,1)} async-done(((bf16[2,256,2048]{2,1,0:T(8,128)(2,1)}), bf16[2,256,256]{2,1,0:T(8,128)(2,1)}) %reduce-scatter.19.cloned.1.call-update) | async-done | bytes 262160 | tf_op jit(solution)/shard_map/while/body/eval_jaxpr/reduce_scatter | solution.py:179
  2104.5 39.6 %reduce-scatter.19.cloned.1.call-done = bf16[2,256,256]{2,1,0:T(8,128)(2,1)} async-done(((bf16[2,256,2048]{2,1,0:T(8,128)(2,1)}), bf16[2,256,256]{2,1,0:T(8,128)(2,1)}) %reduce-scatter.19.cloned.1.call-update) | async-done | bytes 262160 | tf_op jit(solution)/shard_map/while/body/eval_jaxpr/reduce_scatter | solution.py:179
  2180.3 39.6 %reduce-scatter.19.cloned.1.call-done = bf16[2,256,256]{2,1,0:T(8,128)(2,1)} async-done(((bf16[2,256,2048]{2,1,0:T(8,128)(2,1)}), bf16[2,256,256]{2,1,0:T(8,128)(2,1)}) %reduce-scatter.19.cloned.1.call-update) | async-done | bytes 262160 | tf_op jit(solution)/shard_map/while/body/eval_jaxpr/reduce_scatter | solution.py:179
  2256.1 39.6 %reduce-scatter.19.cloned.1.call-done = bf16[2,256,256]{2,1,0:T(8,128)(2,1)} async-done(((bf16[2,256,2048]{2,1,0:T(8,128)(2,1)}), bf16[2,256,256]{2,1,0:T(8,128)(2,1)}) %reduce-scatter.19.cloned.1.call-update) | async-done | bytes 262160 | tf_op jit(solution)/shard_map/while/body/eval_jaxpr/reduce_scatter | solution.py:179
  2331.8 39.7 %reduce-scatter.19.cloned.1.call-done = bf16[2,256,256]{2,1,0:T(8,128)(2,1)} async-done(((bf16[2,256,2048]{2,1,0:T(8,128)(2,1)}), bf16[2,256,256]{2,1,0:T(8,128)(2,1)}) %reduce-scatter.19.cloned.1.call-update) | async-done | bytes 262160 | tf_op jit(solution)/shard_map/while/body/eval_jaxpr/reduce_scatter | solution.py:179
  2407.6 39.7 %reduce-scatter.19.cloned.1.call-done = bf16[2,256,256]{2,1,0:T(8,128)(2,1)} async-done(((bf16[2,256,2048]{2,1,0:T(8,128)(2,1)}), bf16[2,256,256]{2,1,0:T(8,128)(2,1)}) %reduce-scatter.19.cloned.1.call-update) | async-done | bytes 262160 | tf_op jit(solution)/shard_map/while/body/eval_jaxpr/reduce_scatter | solution.py:179
  2483.4 39.7 %reduce-scatter.19.cloned.1.call-done = bf16[2,256,256]{2,1,0:T(8,128)(2,1)} async-done(((bf16[2,256,2048]{2,1,0:T(8,128)(2,1)}), bf16[2,256,256]{2,1,0:T(8,128)(2,1)}) %reduce-scatter.19.cloned.1.call-update) | async-done | bytes 262160 | tf_op jit(solution)/shard_map/while/body/eval_jaxpr/reduce_scatter | solution.py:179
  2559.2 39.7 %reduce-scatter.19.cloned.1.call-done = bf16[2,256,256]{2,1,0:T(8,128)(2,1)} async-done(((bf16[2,256,2048]{2,1,0:T(8,128)(2,1)}), bf16[2,256,256]{2,1,0:T(8,128)(2,1)}) %reduce-scatter.19.cloned.1.call-update) | async-done | bytes 262160 | tf_op jit(solution)/shard_map/while/body/eval_jaxpr/reduce_scatter | solution.py:179
  2635.0 39.7 %reduce-scatter.19.cloned.1.call-done = bf16[2,256,256]{2,1,0:T(8,128)(2,1)} async-done(((bf16[2,256,2048]{2,1,0:T(8,128)(2,1)}), bf16[2,256,256]{2,1,0:T(8,128)(2,1)}) %reduce-scatter.19.cloned.1.call-update) | async-done | bytes 262160 | tf_op jit(solution)/shard_map/while/body/eval_jaxpr/reduce_scatter | solution.py:179
  2710.9 39.6 %reduce-scatter.19.cloned.1.call-done = bf16[2,256,256]{2,1,0:T(8,128)(2,1)} async-done(((bf16[2,256,2048]{2,1,0:T(8,128)(2,1)}), bf16[2,256,256]{2,1,0:T(8,128)(2,1)}) %reduce-scatter.19.cloned.1.call-update) | async-done | bytes 262160 | tf_op jit(solution)/shard_map/while/body/eval_jaxpr/reduce_scatter | solution.py:179
  2753.0 41.4 %copy.215 = bf16[16,2,256,1024]{3,2,0,1:T(8,128)(2,1)} copy(bf16[16,2,256,1024]{2,1,3,0:T(2,128)(2,1)} %get-tuple-element.370) | data formatting | bytes 33554432 | tf_op jit(solution)/shard_map/while | solution.py:185
  2794.4 11.6 slice_bitcast_fusion.5
  2806.0 8.0 reverse_bitcast_fusion
  2814.0 8.9 pad_maximum_fusion
  2822.9 8.9 copy.217
  2846.8 18.8 reduce_sum.97
  2865.7 347.0 %all-to-all-done.3 = bf16[16,256,2,1024]{3,1,2,0:T(8,128)(2,1)} async-done(((bf16[16,256,2,1024]{3,1,2,0:T(8,128)(2,1)}), bf16[16,256,2,1024]{3,1,2,0:T(8,128)(2,1)}, u32[]{:S(2)}, u32[]{:S(2)}) %all-to-all-start.3) | async-done | bytes 16777248 | tf_op jit(solution)/shard_map/all_to_all | solution.py:196
  3212.7 8.2 copy.218
  3229.3 9.2 fusion.46
  3238.5 42.5 %bitcast_convert_fusion = bf16[2,2048,1024]{2,1,0:T(8,128)(2,1)} fusion(bf16[16,2,256,2048]{2,3,0,1:T(8,128)(2,1)} %all-gather.6.cloned.1.call-done, bf16[16,2,256,1024]{3,2,0,1:T(8,128)(2,1)} %copy.215), kind=kOutput, calls=%fused_computation.73 | convolution fusion | flops 34363932672 | bytes 58720256 | tf_op jit(solution)/shard_map/sdbh,sdbc->dhc/dot_general | solution.py:188
  3287.2 37.6 %all-reduce = (f32[]{:T(128)}, f32[2,275]{1,0:T(2,128)}, f32[2]{0:T(128)S(1)}, f32[2]{0:T(128)S(1)}) all-reduce(f32[]{:T(128)} %get-tuple-element.605, f32[2,275]{1,0:T(2,128)S(1)} %copy-done.25, f32[2]{0:T(128)S(1)} %fusion.27, f32[2]{0:T(128)S(1)} %copy-done.26), channel_id=1, replica_groups=mesh['seq'=4,'mp'=8] {'seq','mp'}, use_global_device_ids=true, to_apply=%region_7.8 | all-reduce | flops 555 | bytes 4440 | tf_op jit(solution)/shard_map/psum | solution.py:220
  3329.6 23.4 all-reduce.3.cloned.1.call-done
  3354.8 22.2 reduce-scatter.11.cloned.1.call-done
  3378.7 143.3 %reduce-scatter.13.cloned.1.call-done = bf16[2,512,1024]{2,1,0:T(8,128)(2,1)} async-done(((bf16[2,2048,1024]{2,1,0:T(8,128)(2,1)}), bf16[2,512,1024]{2,1,0:T(8,128)(2,1)}) %reduce-scatter.13.cloned.1.call-update) | async-done | bytes 2097168 | tf_op jit(solution)/shard_map/reduce_scatter | solution.py:207
  (1008 shorter events, 989.5 us)
Async XLA Ops:
  8.0 19.3 copy-start
  8.9 12.1 collective-permute-start
  13.8 7.2 collective-permute-start.1
  21.0 44.0 %copy-start.20 = (s32[1024]{0:T(1024)}, s32[1024]{0:T(1024)S(1)}, u32[]{:S(2)}) copy-start(s32[1024]{0:T(1024)S(1)} %get-tuple-element.603) | copy-start | bytes 12292
  57.6 370.8 %all-to-all-start = ((bf16[4,1024,2,1024]{3,0,2,1:T(4,128)(2,1)}), bf16[4,1024,2,1024]{3,0,2,1:T(4,128)(2,1)}, u32[]{:S(2)}, u32[]{:S(2)}) async-start(bf16[4,1024,2,1024]{3,0,2,1:T(4,128)(2,1)} %copy.204), calls=%async_computation.1 | async-start | bytes 33554432 | tf_op jit(solution)/shard_map/all_to_all | solution.py:70
  446.0 30.5 all-gather.8.cloned.1.call-start
  493.2 31.5 all-gather.8.cloned.1.call-start
  541.4 31.5 all-gather.8.cloned.1.call-start
  589.6 31.2 all-gather.8.cloned.1.call-start
  637.5 31.2 all-gather.8.cloned.1.call-start
  685.4 31.2 all-gather.8.cloned.1.call-start
  733.3 31.5 all-gather.8.cloned.1.call-start
  781.4 31.5 all-gather.8.cloned.1.call-start
  829.5 31.5 all-gather.8.cloned.1.call-start
  877.7 31.2 all-gather.8.cloned.1.call-start
  925.5 31.5 all-gather.8.cloned.1.call-start
  973.8 31.2 all-gather.8.cloned.1.call-start
  1021.6 31.5 all-gather.8.cloned.1.call-start
  1069.8 31.2 all-gather.8.cloned.1.call-start
  1117.7 31.2 all-gather.8.cloned.1.call-start
  1165.5 31.2 all-gather.8.cloned.1.call-start
  1213.3 158.6 %reduce-scatter.9.cloned.1.call-start = ((), (), s32[]{:S(2)}) async-start(), calls=%async_computation.10 | async-start | bytes 5160960 | tf_op jit(solution)/shard_map/reduce_scatter | solution.py:111
  1320.5 51.4 %copy-start.19 = (f32[2,275]{1,0:T(2,128)S(1)}, f32[2,275]{1,0:T(2,128)}, u32[]{:S(2)}) copy-start(f32[2,275]{1,0:T(2,128)} %param.25) | copy-start | bytes 6604
  1320.6 97.7 %all-gather.4.cloned.1.call-start = ((), (), s32[]{:S(2)}) async-start(), calls=%async_computation.11 | async-start | bytes 5160960 | tf_op jit(solution)/shard_map/all_gather | solution.py:147
  1426.0 98.8 %all-to-all-start.2 = ((bf16[4,4,256,2,256]{4,2,1,3,0:T(8,128)(2,1)}), bf16[4,4,256,2,256]{4,2,1,3,0:T(8,128)(2,1)}, u32[]{:S(2)}, u32[]{:S(2)}) async-start(bf16[4,4,256,2,256]{4,2,1,3,0:T(8,128)(2,1)} %pad_maximum_fusion.2), calls=%async_computation.4 | async-start | bytes 8388608 | tf_op jit(solution)/shard_map/all_to_all | solution.py:10
  1541.9 71.7 %reduce-scatter.19.cloned.1.call-start = ((), (), s32[]{:S(2)}) async-start(), calls=%async_computation.19 | async-start | bytes 2359296 | tf_op jit(solution)/shard_map/while/body/eval_jaxpr/reduce_scatter | solution.py:179
  1574.1 39.5 %copy-start.14 = (pred[2,256]{1,0:T(4,128)(4,1)S(1)}, pred[2,256]{1,0:T(4,128)(4,1)}, u32[]{:S(2)}) copy-start(pred[2,256]{1,0:T(4,128)(4,1)} %copy-done.13) | copy-start | bytes 1540 | tf_op jit(solution)/shard_map/while
  1615.5 73.9 %reduce-scatter.19.cloned.1.call-start = ((), (), s32[]{:S(2)}) async-start(), calls=%async_computation.19 | async-start | bytes 2359296 | tf_op jit(solution)/shard_map/while/body/eval_jaxpr/reduce_scatter | solution.py:179
  1648.0 41.4 %copy-start.14 = (pred[2,256]{1,0:T(4,128)(4,1)S(1)}, pred[2,256]{1,0:T(4,128)(4,1)}, u32[]{:S(2)}) copy-start(pred[2,256]{1,0:T(4,128)(4,1)} %copy-done.13) | copy-start | bytes 1540 | tf_op jit(solution)/shard_map/while
  1691.3 73.9 %reduce-scatter.19.cloned.1.call-start = ((), (), s32[]{:S(2)}) async-start(), calls=%async_computation.19 | async-start | bytes 2359296 | tf_op jit(solution)/shard_map/while/body/eval_jaxpr/reduce_scatter | solution.py:179
  1723.8 41.4 %copy-start.14 = (pred[2,256]{1,0:T(4,128)(4,1)S(1)}, pred[2,256]{1,0:T(4,128)(4,1)}, u32[]{:S(2)}) copy-start(pred[2,256]{1,0:T(4,128)(4,1)} %copy-done.13) | copy-start | bytes 1540 | tf_op jit(solution)/shard_map/while
  1767.1 73.9 %reduce-scatter.19.cloned.1.call-start = ((), (), s32[]{:S(2)}) async-start(), calls=%async_computation.19 | async-start | bytes 2359296 | tf_op jit(solution)/shard_map/while/body/eval_jaxpr/reduce_scatter | solution.py:179
  1799.6 41.4 %copy-start.14 = (pred[2,256]{1,0:T(4,128)(4,1)S(1)}, pred[2,256]{1,0:T(4,128)(4,1)}, u32[]{:S(2)}) copy-start(pred[2,256]{1,0:T(4,128)(4,1)} %copy-done.13) | copy-start | bytes 1540 | tf_op jit(solution)/shard_map/while
  1842.9 73.9 %reduce-scatter.19.cloned.1.call-start = ((), (), s32[]{:S(2)}) async-start(), calls=%async_computation.19 | async-start | bytes 2359296 | tf_op jit(solution)/shard_map/while/body/eval_jaxpr/reduce_scatter | solution.py:179
  1875.4 41.4 %copy-start.14 = (pred[2,256]{1,0:T(4,128)(4,1)S(1)}, pred[2,256]{1,0:T(4,128)(4,1)}, u32[]{:S(2)}) copy-start(pred[2,256]{1,0:T(4,128)(4,1)} %copy-done.13) | copy-start | bytes 1540 | tf_op jit(solution)/shard_map/while
  1918.7 73.9 %reduce-scatter.19.cloned.1.call-start = ((), (), s32[]{:S(2)}) async-start(), calls=%async_computation.19 | async-start | bytes 2359296 | tf_op jit(solution)/shard_map/while/body/eval_jaxpr/reduce_scatter | solution.py:179
  1951.2 41.4 %copy-start.14 = (pred[2,256]{1,0:T(4,128)(4,1)S(1)}, pred[2,256]{1,0:T(4,128)(4,1)}, u32[]{:S(2)}) copy-start(pred[2,256]{1,0:T(4,128)(4,1)} %copy-done.13) | copy-start | bytes 1540 | tf_op jit(solution)/shard_map/while
  1994.5 73.9 %reduce-scatter.19.cloned.1.call-start = ((), (), s32[]{:S(2)}) async-start(), calls=%async_computation.19 | async-start | bytes 2359296 | tf_op jit(solution)/shard_map/while/body/eval_jaxpr/reduce_scatter | solution.py:179
  2027.0 41.4 %copy-start.14 = (pred[2,256]{1,0:T(4,128)(4,1)S(1)}, pred[2,256]{1,0:T(4,128)(4,1)}, u32[]{:S(2)}) copy-start(pred[2,256]{1,0:T(4,128)(4,1)} %copy-done.13) | copy-start | bytes 1540 | tf_op jit(solution)/shard_map/while
  2070.2 73.9 %reduce-scatter.19.cloned.1.call-start = ((), (), s32[]{:S(2)}) async-start(), calls=%async_computation.19 | async-start | bytes 2359296 | tf_op jit(solution)/shard_map/while/body/eval_jaxpr/reduce_scatter | solution.py:179
  2102.8 41.4 %copy-start.14 = (pred[2,256]{1,0:T(4,128)(4,1)S(1)}, pred[2,256]{1,0:T(4,128)(4,1)}, u32[]{:S(2)}) copy-start(pred[2,256]{1,0:T(4,128)(4,1)} %copy-done.13) | copy-start | bytes 1540 | tf_op jit(solution)/shard_map/while
  2146.0 73.9 %reduce-scatter.19.cloned.1.call-start = ((), (), s32[]{:S(2)}) async-start(), calls=%async_computation.19 | async-start | bytes 2359296 | tf_op jit(solution)/shard_map/while/body/eval_jaxpr/reduce_scatter | solution.py:179
  2178.5 41.4 %copy-start.14 = (pred[2,256]{1,0:T(4,128)(4,1)S(1)}, pred[2,256]{1,0:T(4,128)(4,1)}, u32[]{:S(2)}) copy-start(pred[2,256]{1,0:T(4,128)(4,1)} %copy-done.13) | copy-start | bytes 1540 | tf_op jit(solution)/shard_map/while
  2221.8 73.9 %reduce-scatter.19.cloned.1.call-start = ((), (), s32[]{:S(2)}) async-start(), calls=%async_computation.19 | async-start | bytes 2359296 | tf_op jit(solution)/shard_map/while/body/eval_jaxpr/reduce_scatter | solution.py:179
  2254.3 41.4 %copy-start.14 = (pred[2,256]{1,0:T(4,128)(4,1)S(1)}, pred[2,256]{1,0:T(4,128)(4,1)}, u32[]{:S(2)}) copy-start(pred[2,256]{1,0:T(4,128)(4,1)} %copy-done.13) | copy-start | bytes 1540 | tf_op jit(solution)/shard_map/while
  2297.6 73.9 %reduce-scatter.19.cloned.1.call-start = ((), (), s32[]{:S(2)}) async-start(), calls=%async_computation.19 | async-start | bytes 2359296 | tf_op jit(solution)/shard_map/while/body/eval_jaxpr/reduce_scatter | solution.py:179
  2330.1 41.4 %copy-start.14 = (pred[2,256]{1,0:T(4,128)(4,1)S(1)}, pred[2,256]{1,0:T(4,128)(4,1)}, u32[]{:S(2)}) copy-start(pred[2,256]{1,0:T(4,128)(4,1)} %copy-done.13) | copy-start | bytes 1540 | tf_op jit(solution)/shard_map/while
  2373.4 73.9 %reduce-scatter.19.cloned.1.call-start = ((), (), s32[]{:S(2)}) async-start(), calls=%async_computation.19 | async-start | bytes 2359296 | tf_op jit(solution)/shard_map/while/body/eval_jaxpr/reduce_scatter | solution.py:179
  2405.9 41.4 %copy-start.14 = (pred[2,256]{1,0:T(4,128)(4,1)S(1)}, pred[2,256]{1,0:T(4,128)(4,1)}, u32[]{:S(2)}) copy-start(pred[2,256]{1,0:T(4,128)(4,1)} %copy-done.13) | copy-start | bytes 1540 | tf_op jit(solution)/shard_map/while
  2449.2 73.9 %reduce-scatter.19.cloned.1.call-start = ((), (), s32[]{:S(2)}) async-start(), calls=%async_computation.19 | async-start | bytes 2359296 | tf_op jit(solution)/shard_map/while/body/eval_jaxpr/reduce_scatter | solution.py:179
  2481.7 41.4 %copy-start.14 = (pred[2,256]{1,0:T(4,128)(4,1)S(1)}, pred[2,256]{1,0:T(4,128)(4,1)}, u32[]{:S(2)}) copy-start(pred[2,256]{1,0:T(4,128)(4,1)} %copy-done.13) | copy-start | bytes 1540 | tf_op jit(solution)/shard_map/while
  2525.0 73.9 %reduce-scatter.19.cloned.1.call-start = ((), (), s32[]{:S(2)}) async-start(), calls=%async_computation.19 | async-start | bytes 2359296 | tf_op jit(solution)/shard_map/while/body/eval_jaxpr/reduce_scatter | solution.py:179
  2557.5 41.4 %copy-start.14 = (pred[2,256]{1,0:T(4,128)(4,1)S(1)}, pred[2,256]{1,0:T(4,128)(4,1)}, u32[]{:S(2)}) copy-start(pred[2,256]{1,0:T(4,128)(4,1)} %copy-done.13) | copy-start | bytes 1540 | tf_op jit(solution)/shard_map/while
  2600.8 73.9 %reduce-scatter.19.cloned.1.call-start = ((), (), s32[]{:S(2)}) async-start(), calls=%async_computation.19 | async-start | bytes 2359296 | tf_op jit(solution)/shard_map/while/body/eval_jaxpr/reduce_scatter | solution.py:179
  2633.3 41.4 %copy-start.14 = (pred[2,256]{1,0:T(4,128)(4,1)S(1)}, pred[2,256]{1,0:T(4,128)(4,1)}, u32[]{:S(2)}) copy-start(pred[2,256]{1,0:T(4,128)(4,1)} %copy-done.13) | copy-start | bytes 1540 | tf_op jit(solution)/shard_map/while
  2676.6 73.9 %reduce-scatter.19.cloned.1.call-start = ((), (), s32[]{:S(2)}) async-start(), calls=%async_computation.19 | async-start | bytes 2359296 | tf_op jit(solution)/shard_map/while/body/eval_jaxpr/reduce_scatter | solution.py:179
  2709.1 41.4 %copy-start.14 = (pred[2,256]{1,0:T(4,128)(4,1)S(1)}, pred[2,256]{1,0:T(4,128)(4,1)}, u32[]{:S(2)}) copy-start(pred[2,256]{1,0:T(4,128)(4,1)} %copy-done.13) | copy-start | bytes 1540 | tf_op jit(solution)/shard_map/while
  2752.4 486.1 %all-gather.6.cloned.1.call-start = ((), (), s32[]{:S(2)}) async-start(), calls=%async_computation.14 | async-start | bytes 37748736 | tf_op jit(solution)/shard_map/all_gather | solution.py:190
  2831.7 381.0 %all-to-all-start.3 = ((bf16[16,256,2,1024]{3,1,2,0:T(8,128)(2,1)}), bf16[16,256,2,1024]{3,1,2,0:T(8,128)(2,1)}, u32[]{:S(2)}, u32[]{:S(2)}) async-start(bf16[16,256,2,1024]{3,1,2,0:T(8,128)(2,1)} %copy.217), calls=%async_computation.5 | async-start | bytes 33554432 | tf_op jit(solution)/shard_map/all_to_all | solution.py:196
  2839.0 487.5 %reduce-scatter.15.cloned.1.call-start = ((), (), s32[]{:S(2)}) async-start(), calls=%async_computation.16 | async-start | bytes 491520 | tf_op jit(solution)/shard_map/reduce_scatter | solution.py:216
  2846.8 481.3 %reduce-scatter.17.cloned.1.call-start = ((), (), s32[]{:S(2)}) async-start(), calls=%async_computation.17 | async-start | bytes 327680
  2865.7 487.3 %all-reduce.3.cloned.1.call-start = ((), (), s32[]{:S(2)}) async-start(), calls=%async_computation.12 | async-start | bytes 573440 | tf_op jit(solution)/shard_map/psum | solution.py:220
  3229.0 148.0 %reduce-scatter.11.cloned.1.call-start = ((), (), s32[]{:S(2)}) async-start(), calls=%async_computation.13 | async-start | bytes 532480 | tf_op jit(solution)/shard_map/reduce_scatter | solution.py:213
  3238.5 283.5 %reduce-scatter.13.cloned.1.call-start = ((), (), s32[]{:S(2)}) async-start(), calls=%async_computation.15 | async-start | bytes 10485760 | tf_op jit(solution)/shard_map/reduce_scatter | solution.py:207
  (83 other events, 381.3 us)
Sparse Core Ops, SparseCore 0:
  449.3 27.1 all-gather.7
  496.5 28.1 all-gather.7
  544.7 28.1 all-gather.7
  592.6 28.1 all-gather.7
  640.5 28.1 all-gather.7
  688.3 28.1 all-gather.7
  736.6 28.1 all-gather.7
  784.7 28.1 all-gather.7
  832.8 28.1 all-gather.7
  880.7 28.1 all-gather.7
  928.8 28.1 all-gather.7
  976.7 28.1 all-gather.7
  1024.9 28.1 all-gather.7
  1072.8 28.1 all-gather.7
  1120.7 28.1 all-gather.7
  1168.5 28.1 all-gather.7
  1574.2 39.3 reduce-scatter.18
  1648.2 41.2 reduce-scatter.18
  1724.0 41.2 reduce-scatter.18
  1799.7 41.2 reduce-scatter.18
  1875.5 41.2 reduce-scatter.18
  1951.3 41.2 reduce-scatter.18
  2027.1 41.2 reduce-scatter.18
  2102.9 41.2 reduce-scatter.18
  2178.7 41.2 reduce-scatter.18
  2254.5 41.2 reduce-scatter.18
  2330.3 41.2 reduce-scatter.18
  2406.1 41.2 reduce-scatter.18
  2481.8 41.2 reduce-scatter.18
  2557.6 41.2 reduce-scatter.18
  2633.4 41.2 reduce-scatter.18
  2709.3 41.2 reduce-scatter.18
Sparse Core Ops, SparseCore 1:
  1320.7 51.3 reduce-scatter.8
  1379.2 38.9 all-gather.3
  2755.4 160.6 all-gather.5
  2918.3 28.0 reduce-scatter.14
  2949.4 191.9 reduce-scatter.16
  3229.1 123.8 all-reduce.2
  3355.2 21.7 reduce-scatter.10
  3379.2 142.7 reduce-scatter.12
